TPU v7x, 32 devices: a whole 2x2x4 slice. The times are simulated.
32 devices in a mesh: face: 2 (over y), ty: 4 (over x, core), tx: 4 (over z).
Axes of the slice: x: 2, y: 2, z: 4, core: 2. Of those that a mesh axis runs over, the one named last changes fastest.
Arguments:
- cotangent: float32 [2, 32, 32, 128], P('face', 'ty', 'tx'), may hold values from -6 to 6
- courant_x: float32 [2, 32, 36, 32], P('face', 'ty', 'tx'), may hold values from -0.6 to 0.6
- edge_x: float32 [2, 32, 36], P('face', 'ty', 'tx'), may hold values from 0.7 to 1.4
- courant_y: float32 [2, 36, 32, 32], P('face', 'ty', 'tx'), may hold values from -0.6 to 0.6
- edge_y: float32 [2, 36, 32], P('face', 'ty', 'tx'), may hold values from 0.7 to 1.4
- cell_area: float32 [2, 32, 32], P('face', 'ty', 'tx'), may hold values from 0.7 to 1.4
- seam_partner: int32 [2, 4], replicated, may hold values from 0 to 7, as said below
- seam_flip: int32 [2, 4], replicated, may hold values from 0 to 1, as said below
Outputs:
- sensitivity: float32 [2, 32, 32, 128], P('face', 'ty', 'tx')
Inputs may be any that keep to these rules, and one draw needn't show every extreme that they name: `seam_partner`: the gluing pairs face edges: the partner of an edge's partner is that edge, and no edge is glued to itself; some east or west edge is glued to a north or south edge. `seam_flip`: the same for both edges of a glued pair.
All inputs are finite; a program needn't handle non-finite values.
Results may differ from a plain program's by a relative error of at most 0.0003.
Values sent between devices are 32-bit elements; how exact they have to be, the bound alone decides.
No kernel may reach another device: no remote copies, remote signals or barrier semaphores. Data moves between devices by JAX's collectives and lax.ppermute only.
A program may use at most 64 MiB of HBM per device.

v0:
```python
import jax
import jax.numpy as jnp
from jax import lax
from jax.sharding import PartitionSpec as P

STEPS = 2


def padded(cells, sides, width):
    for axis, dim in sides:
        count = lax.axis_size(axis)
        ends = count - 1
        head = lax.slice_in_dim(cells, 0, width, axis=dim)
        tail = lax.slice_in_dim(cells, cells.shape[dim] - width, cells.shape[dim], axis=dim)
        cells = jnp.concatenate(
            [
                lax.ppermute(tail, axis, [(i, (i + 1) % count) for i in range(ends)]),
                cells,
                lax.ppermute(head, axis, [((i + 1) % count, i) for i in range(ends)]),
            ],
            axis=dim,
        )
    return cells


def take_slab(source, axis_at, anchor, finish):
    return lax.slice_in_dim(source, anchor, finish, axis=axis_at)


def parabolic_sweep(extended, courant, edge_length, area_cells, axis_at):
    inner_count = extended.shape[axis_at] - 6
    interface_value = 7.0 / 12.0 * (
        take_slab(extended, axis_at, 1, inner_count + 4)
        + take_slab(extended, axis_at, 2, inner_count + 5)
    ) - 1.0 / 12.0 * (
        take_slab(extended, axis_at, 0, inner_count + 3)
        + take_slab(extended, axis_at, 3, inner_count + 6)
    )
    a_low = take_slab(interface_value, axis_at, 0, inner_count + 1)
    a_mid = take_slab(interface_value, axis_at, 1, inner_count + 2)
    a_high = take_slab(interface_value, axis_at, 2, inner_count + 3)
    left_cell = take_slab(extended, axis_at, 2, inner_count + 3)
    right_cell = take_slab(extended, axis_at, 3, inner_count + 4)
    curve_left = 6.0 * left_cell - 3.0 * (a_low + a_mid)
    curve_right = 6.0 * right_cell - 3.0 * (a_mid + a_high)
    upwind = -courant
    from_left = a_mid - 0.5 * courant * (a_mid - a_low - (1.0 - courant * (2.0 / 3.0)) * curve_left)
    from_right = a_mid + 0.5 * upwind * (
        a_high - a_mid + (1.0 - upwind * (2.0 / 3.0)) * curve_right
    )
    face_value = jnp.where(courant > 0, from_left, from_right)
    flux_term = courant * edge_length * face_value
    return (
        take_slab(extended, axis_at, 3, inner_count + 3)
        - (
            take_slab(flux_term, axis_at, 1, inner_count + 1)
            - take_slab(flux_term, axis_at, 0, inner_count)
        )
        / area_cells
    )


def indicator(flag):
    return flag.astype(jnp.float32)


def on_device(cotangent, courant_x, edge_x, courant_y, edge_y, cell_area, seam_partner, seam_flip):
    adjoint = cotangent[0]
    height_cells, width_cells, lanes_all = adjoint.shape
    repeat_count = lanes_all // courant_x.shape[-1]
    tiles_wide = lax.axis_size("tx")
    tiles_high = lax.axis_size("ty")
    face_index = lax.axis_index("face")
    row_index = lax.axis_index("ty")
    column_index = lax.axis_index("tx")
    spread_x = jnp.tile(courant_x[0], repeat_count)
    length_x = edge_x[0][:, :, None]
    spread_y = jnp.tile(courant_y[0], repeat_count)
    length_y = edge_y[0][:, :, None]
    area_cells = cell_area[0][:, :, None]
    own_codes = lax.dynamic_index_in_dim(seam_partner, face_index, 0, keepdims=False)
    own_flips = lax.dynamic_index_in_dim(seam_flip, face_index, 0, keepdims=False)
    on_east = indicator(column_index == tiles_wide - 1)
    on_west = indicator(column_index == 0)
    on_north = indicator(row_index == tiles_high - 1)
    on_south = indicator(row_index == 0)

    def deliver(strips, parity):
        gathered = lax.all_gather(strips[None], "face", axis=0, tiled=True)
        result = jnp.zeros((height_cells, width_cells, lanes_all), jnp.float32)
        for border in range(4):
            code = own_codes[border]
            other_face = code // 4
            other_border = code % 4
            active = indicator(other_border % 2 == parity)
            chosen = lax.dynamic_index_in_dim(gathered, other_face, 0, keepdims=False)
            chosen = lax.dynamic_index_in_dim(chosen, other_border // 2, 0, keepdims=False)
            chosen = jnp.where(own_flips[border] == 1, chosen[:, ::-1], chosen)
            if border == 0 or border == 2:
                segment = lax.dynamic_slice_in_dim(
                    chosen, row_index * height_cells, height_cells, 1
                )
                columns = jnp.swapaxes(segment, 0, 1)
                if border == 0:
                    result = result.at[:, width_cells - 3 :].add(
                        columns[:, ::-1] * (active * on_east)
                    )
                else:
                    result = result.at[:, :3].add(columns * (active * on_west))
            else:
                segment = lax.dynamic_slice_in_dim(
                    chosen, column_index * width_cells, width_cells, 1
                )
                if border == 1:
                    result = result.at[height_cells - 3 :].add(segment[::-1] * (active * on_north))
                else:
                    result = result.at[:3].add(segment * (active * on_south))
        return result

    def reverse_x(current):
        blank = jnp.zeros((height_cells, width_cells + 6, lanes_all), jnp.float32)

        def sweep_x(extended):
            return parabolic_sweep(extended, spread_x, length_x, area_cells, 1)

        unused, pullback = jax.vjp(sweep_x, blank)
        halo_adjoint = pullback(current)[0]
        own_part = halo_adjoint[:, 3 : width_cells + 3]
        west_rim = halo_adjoint[:, :3]
        east_rim = halo_adjoint[:, width_cells + 3 :]
        packed = jnp.concatenate([west_rim, east_rim], axis=1)
        bordered = padded(packed, (("tx", 1),), 3)
        own_part = (
            own_part.at[:, :3].add(bordered[:, :3]).at[:, width_cells - 3 :].add(bordered[:, 9:])
        )
        east_piece = jnp.swapaxes(east_rim, 0, 1) * on_east
        west_piece = jnp.swapaxes(west_rim[:, ::-1], 0, 1) * on_west
        pieces = jnp.stack([east_piece, west_piece])
        row_total = lax.psum(pieces, "tx")
        strips = lax.all_gather(row_total, "ty", axis=2, tiled=True)
        return own_part + deliver(strips, 0)

    def reverse_y(current):
        blank = jnp.zeros((height_cells + 6, width_cells, lanes_all), jnp.float32)

        def sweep_y(extended):
            return parabolic_sweep(extended, spread_y, length_y, area_cells, 0)

        unused, pullback = jax.vjp(sweep_y, blank)
        halo_adjoint = pullback(current)[0]
        own_part = halo_adjoint[3 : height_cells + 3]
        south_rim = halo_adjoint[:3]
        north_rim = halo_adjoint[height_cells + 3 :]
        packed = jnp.concatenate([south_rim, north_rim], axis=0)
        bordered = padded(packed, (("ty", 0),), 3)
        own_part = own_part.at[:3].add(bordered[:3]).at[height_cells - 3 :].add(bordered[9:])
        north_piece = north_rim * on_north
        south_piece = south_rim[::-1] * on_south
        pieces = jnp.stack([north_piece, south_piece])
        column_total = lax.psum(pieces, "ty")
        strips = lax.all_gather(column_total, "tx", axis=2, tiled=True)
        return own_part + deliver(strips, 1)

    for repeat in range(STEPS):
        adjoint = reverse_y(adjoint)
        adjoint = reverse_x(adjoint)
    return adjoint[None]


def solution(mesh):
    placed = (
        P("face", "ty", "tx", None),
        P("face", "ty", "tx", None),
        P("face", "ty", "tx"),
        P("face", "ty", "tx", None),
        P("face", "ty", "tx"),
        P("face", "ty", "tx"),
        P(),
        P(),
    )
    return jax.shard_map(
        on_device,
        mesh=mesh,
        in_specs=placed,
        out_specs=P("face", "ty", "tx", None),
        check_vma=False,
    )
```

profile of v0, /device:TPU:0, one launch (start us, length us, event | category | flops | bytes accessed | tf_op | source)
XLA Modules:
  0.0 164.9 jit_solution(16922162289223766744)
XLA Ops:
  0.0 0.8 copy.66
  0.8 0.8 tile.21
  1.6 0.1 tile.22
  1.7 0.6 copy-done
  2.4 0.7 copy-done.2
  3.1 0.1 fusion.17
  3.4 2.4 %collective-permute-start = (f32[3,8,128]{2,0,1:T(4,128)S(1)}, f32[3,8,128]{2,0,1:T(4,128)S(1)}, u32[]{:S(2)}, u32[]{:S(2)}) collective-permute-start(f32[3,8,128]{2,0,1:T(4,128)S(1)} %get-tuple-element.367), channel_id=1, source_target_pairs={{0,4},{4,8},{8,12},{1,5},{5,9},{9,13},{2,6},{6,10},{10,14},{3,7},{... | collective-permute-start | bytes 36872 | tf_op jit(solution)/shard_map/ppermute | solution.py:17
  5.8 1.3 collective-permute-start.1
  7.1 0.7 copy-done.4
  7.8 0.7 fusion.70
  19.3 13.4 %psum.28 = f32[2,3,8,128]{3,1,2,0:T(4,128)S(1)} all-reduce(f32[2,3,8,128]{3,1,2,0:T(4,128)S(1)} %pad_maximum_fusion), channel_id=1, replica_groups=mesh['face'=2,'ty'=4,'tx'=4] {'ty'}, use_global_device_ids=true, to_apply=%region_0.1 | all-reduce | flops 6144 | bytes 49152 | tf_op jit(solution)/shard_map/psum | solution.py:160
  32.7 13.6 %all_gather.24 = f32[2,3,32,128]{3,1,2,0:T(4,128)S(1)} all-gather(f32[2,3,8,128]{3,1,2,0:T(4,128)S(1)} %psum.28), channel_id=1, replica_groups=mesh['face'=2,'ty'=4,'tx'=4] {'tx'}, dimensions={2}, use_global_device_ids=true | all-gather | bytes 122880 | tf_op jit(solution)/shard_map/all_gather | solution.py:161
  46.3 5.3 %all-gather = f32[4,3,32,128]{3,2,1,0:T(8,128)S(1)} all-gather(f32[2,3,32,128]{3,2,1,0:T(8,128)S(1)} %copy.69), channel_id=2, replica_groups=mesh['face'=2,'ty'=4,'tx'=4] {'face'}, dimensions={0}, use_global_device_ids=true | all-gather | bytes 294912 | tf_op jit(solution)/shard_map/all_gather | solution.py:89
  51.6 0.7 fusion.69
  55.2 0.1 scatter-add.85
  55.4 0.7 copy-done.1
  56.2 0.1 tile.25
  56.3 0.1 scatter-add.89
  56.5 0.4 copy-done.3
  57.0 0.1 scatter-add.80
  57.1 0.1 scatter-add.81
  57.3 0.1 fusion.67
  57.5 3.5 %collective-permute-start.2 = (f32[8,3,128]{2,0,1:T(8,128)S(1)}, f32[8,3,128]{2,0,1:T(8,128)S(1)}, u32[]{:S(2)}, u32[]{:S(2)}) collective-permute-start(f32[8,3,128]{2,0,1:T(8,128)S(1)} %get-tuple-element.333), channel_id=1, source_target_pairs={{0,1},{1,2},{2,3},{4,5},{5,6},{6,7},{8,9},{9,10},{10,11},{12,13},{... | collective-permute-start | bytes 36872 | tf_op jit(solution)/shard_map/ppermute | solution.py:17
  61.1 1.3 collective-permute-start.3
  62.4 20.3 %psum.29 = f32[2,3,8,128]{3,2,1,0:T(8,128)S(1)} all-reduce(f32[2,3,8,128]{3,2,1,0:T(8,128)S(1)} %pad_maximum_fusion.2), channel_id=1, replica_groups=mesh['face'=2,'ty'=4,'tx'=4] {'tx'}, use_global_device_ids=true, to_apply=%region_1.2 | all-reduce | flops 6144 | bytes 49152 | tf_op jit(solution)/shard_map/psum | solution.py:139
  82.6 5.3 %all_gather.26 = f32[2,3,32,128]{3,2,1,0:T(8,128)S(1)} all-gather(f32[2,3,8,128]{3,2,1,0:T(8,128)S(1)} %psum.29), channel_id=1, replica_groups=mesh['face'=2,'ty'=4,'tx'=4] {'ty'}, dimensions={2}, use_global_device_ids=true | all-gather | bytes 122880 | tf_op jit(solution)/shard_map/all_gather | solution.py:140
  88.0 5.7 %all-gather.1 = f32[4,3,32,128]{3,2,1,0:T(8,128)S(1)} all-gather(f32[2,3,32,128]{3,2,1,0:T(8,128)S(1)} %all_gather.26), channel_id=3, replica_groups=mesh['face'=2,'ty'=4,'tx'=4] {'face'}, dimensions={0}, use_global_device_ids=true | all-gather | bytes 294912 | tf_op jit(solution)/shard_map/all_gather | solution.py:89
  94.0 0.1 scatter-add.95
  94.2 0.1 scatter-add.99
  94.5 0.1 fusion.20
  94.7 1.3 collective-permute-start.5
  96.1 3.0 %collective-permute-start.4 = (f32[3,8,128]{2,0,1:T(4,128)S(1)}, f32[3,8,128]{2,0,1:T(4,128)S(1)}, u32[]{:S(2)}, u32[]{:S(2)}) collective-permute-start(f32[3,8,128]{2,0,1:T(4,128)S(1)} %get-tuple-element.364), channel_id=1, source_target_pairs={{0,4},{4,8},{8,12},{1,5},{5,9},{9,13},{2,6},{6,10},{10,14},{3,7},{... | collective-permute-start | bytes 36872 | tf_op jit(solution)/shard_map/ppermute | solution.py:17
  99.1 11.7 %psum.30 = f32[2,3,8,128]{3,1,2,0:T(4,128)S(1)} all-reduce(f32[2,3,8,128]{3,1,2,0:T(4,128)S(1)} %pad_maximum_fusion.1), channel_id=1, replica_groups=mesh['face'=2,'ty'=4,'tx'=4] {'ty'}, use_global_device_ids=true, to_apply=%region_2.3 | all-reduce | flops 6144 | bytes 49152 | tf_op jit(solution)/shard_map/psum | solution.py:160
  110.8 13.5 %all_gather.28 = f32[2,3,32,128]{3,1,2,0:T(4,128)S(1)} all-gather(f32[2,3,8,128]{3,1,2,0:T(4,128)S(1)} %psum.30), channel_id=1, replica_groups=mesh['face'=2,'ty'=4,'tx'=4] {'tx'}, dimensions={2}, use_global_device_ids=true | all-gather | bytes 122880 | tf_op jit(solution)/shard_map/all_gather | solution.py:161
  124.3 5.3 %all-gather.2 = f32[4,3,32,128]{3,2,1,0:T(8,128)S(1)} all-gather(f32[2,3,32,128]{3,2,1,0:T(8,128)S(1)} %copy.75), channel_id=4, replica_groups=mesh['face'=2,'ty'=4,'tx'=4] {'face'}, dimensions={0}, use_global_device_ids=true | all-gather | bytes 294912 | tf_op jit(solution)/shard_map/all_gather | solution.py:89
  129.9 0.1 scatter-add.105
  130.1 0.1 scatter-add.109
  130.3 0.1 scatter-add.100
  130.4 0.1 scatter-add.101
  130.7 0.1 fusion.30
  130.9 1.3 collective-permute-start.7
  132.2 4.5 %collective-permute-start.6 = (f32[8,3,128]{2,0,1:T(8,128)S(1)}, f32[8,3,128]{2,0,1:T(8,128)S(1)}, u32[]{:S(2)}, u32[]{:S(2)}) collective-permute-start(f32[8,3,128]{2,0,1:T(8,128)S(1)} %get-tuple-element.321), channel_id=1, source_target_pairs={{0,1},{1,2},{2,3},{4,5},{5,6},{6,7},{8,9},{9,10},{10,11},{12,13},{... | collective-permute-start | bytes 36872 | tf_op jit(solution)/shard_map/ppermute | solution.py:17
  136.7 15.8 %psum.31 = f32[2,3,8,128]{3,2,1,0:T(8,128)S(1)} all-reduce(f32[2,3,8,128]{3,2,1,0:T(8,128)S(1)} %pad_maximum_fusion.3), channel_id=1, replica_groups=mesh['face'=2,'ty'=4,'tx'=4] {'tx'}, use_global_device_ids=true, to_apply=%region_3.4 | all-reduce | flops 6144 | bytes 49152 | tf_op jit(solution)/shard_map/psum | solution.py:139
  152.5 5.3 %all_gather.30 = f32[2,3,32,128]{3,2,1,0:T(8,128)S(1)} all-gather(f32[2,3,8,128]{3,2,1,0:T(8,128)S(1)} %psum.31), channel_id=1, replica_groups=mesh['face'=2,'ty'=4,'tx'=4] {'ty'}, dimensions={2}, use_global_device_ids=true | all-gather | bytes 122880 | tf_op jit(solution)/shard_map/all_gather | solution.py:140
  157.8 5.7 %all-gather.3 = f32[4,3,32,128]{3,2,1,0:T(8,128)S(1)} all-gather(f32[2,3,32,128]{3,2,1,0:T(8,128)S(1)} %all_gather.30), channel_id=5, replica_groups=mesh['face'=2,'ty'=4,'tx'=4] {'face'}, dimensions={0}, use_global_device_ids=true | all-gather | bytes 294912 | tf_op jit(solution)/shard_map/all_gather | solution.py:89
  163.8 0.1 scatter-add.115
  164.0 0.1 scatter-add.119
  164.2 0.6 copy.80
  (122 shorter events, 2.1 us)
Async XLA Ops:
  1.6 0.8 copy-start
  2.4 0.7 copy-start.2
  3.4 53.6 %collective-permute-start = (f32[3,8,128]{2,0,1:T(4,128)S(1)}, f32[3,8,128]{2,0,1:T(4,128)S(1)}, u32[]{:S(2)}, u32[]{:S(2)}) collective-permute-start(f32[3,8,128]{2,0,1:T(4,128)S(1)} %get-tuple-element.367), channel_id=1, source_target_pairs={{0,4},{4,8},{8,12},{1,5},{5,9},{9,13},{2,6},{6,10},{10,14},{3,7},{... | collective-permute-start | bytes 36872 | tf_op jit(solution)/shard_map/ppermute | solution.py:17
  5.8 51.4 %collective-permute-start.1 = (f32[3,8,128]{2,0,1:T(4,128)S(1)}, f32[3,8,128]{2,0,1:T(4,128)S(1)}, u32[]{:S(2)}, u32[]{:S(2)}) collective-permute-start(f32[3,8,128]{2,0,1:T(4,128)S(1)} %get-tuple-element.366), channel_id=1, source_target_pairs={{4,0},{8,4},{12,8},{5,1},{9,5},{13,9},{6,2},{10,6},{14,10},{7,3},{... | collective-permute-start | bytes 36872 | tf_op jit(solution)/shard_map/ppermute | solution.py:19
  7.1 0.7 copy-start.4
  7.1 0.7 copy-start.5
  55.4 0.8 copy-start.1
  56.2 0.7 copy-start.3
  57.5 36.8 %collective-permute-start.2 = (f32[8,3,128]{2,0,1:T(8,128)S(1)}, f32[8,3,128]{2,0,1:T(8,128)S(1)}, u32[]{:S(2)}, u32[]{:S(2)}) collective-permute-start(f32[8,3,128]{2,0,1:T(8,128)S(1)} %get-tuple-element.333), channel_id=1, source_target_pairs={{0,1},{1,2},{2,3},{4,5},{5,6},{6,7},{8,9},{9,10},{10,11},{12,13},{... | collective-permute-start | bytes 36872 | tf_op jit(solution)/shard_map/ppermute | solution.py:17
  61.1 33.3 %collective-permute-start.3 = (f32[8,3,128]{2,0,1:T(8,128)S(1)}, f32[8,3,128]{2,0,1:T(8,128)S(1)}, u32[]{:S(2)}, u32[]{:S(2)}) collective-permute-start(f32[8,3,128]{2,0,1:T(8,128)S(1)} %get-tuple-element.307), channel_id=1, source_target_pairs={{1,0},{2,1},{3,2},{5,4},{6,5},{7,6},{9,8},{10,9},{11,10},{13,12},{... | collective-permute-start | bytes 36872 | tf_op jit(solution)/shard_map/ppermute | solution.py:19
  94.7 35.7 %collective-permute-start.5 = (f32[3,8,128]{2,0,1:T(4,128)S(1)}, f32[3,8,128]{2,0,1:T(4,128)S(1)}, u32[]{:S(2)}, u32[]{:S(2)}) collective-permute-start(f32[3,8,128]{2,0,1:T(4,128)S(1)} %get-tuple-element.363), channel_id=1, source_target_pairs={{4,0},{8,4},{12,8},{5,1},{9,5},{13,9},{6,2},{10,6},{14,10},{7,3},{... | collective-permute-start | bytes 36872 | tf_op jit(solution)/shard_map/ppermute | solution.py:19
  96.1 34.2 %collective-permute-start.4 = (f32[3,8,128]{2,0,1:T(4,128)S(1)}, f32[3,8,128]{2,0,1:T(4,128)S(1)}, u32[]{:S(2)}, u32[]{:S(2)}) collective-permute-start(f32[3,8,128]{2,0,1:T(4,128)S(1)} %get-tuple-element.364), channel_id=1, source_target_pairs={{0,4},{4,8},{8,12},{1,5},{5,9},{9,13},{2,6},{6,10},{10,14},{3,7},{... | collective-permute-start | bytes 36872 | tf_op jit(solution)/shard_map/ppermute | solution.py:17
  130.9 33.4 %collective-permute-start.7 = (f32[8,3,128]{2,0,1:T(8,128)S(1)}, f32[8,3,128]{2,0,1:T(8,128)S(1)}, u32[]{:S(2)}, u32[]{:S(2)}) collective-permute-start(f32[8,3,128]{2,0,1:T(8,128)S(1)} %get-tuple-element.295), channel_id=1, source_target_pairs={{1,0},{2,1},{3,2},{5,4},{6,5},{7,6},{9,8},{10,9},{11,10},{13,12},{... | collective-permute-start | bytes 36872 | tf_op jit(solution)/shard_map/ppermute | solution.py:19
  132.2 32.0 %collective-permute-start.6 = (f32[8,3,128]{2,0,1:T(8,128)S(1)}, f32[8,3,128]{2,0,1:T(8,128)S(1)}, u32[]{:S(2)}, u32[]{:S(2)}) collective-permute-start(f32[8,3,128]{2,0,1:T(8,128)S(1)} %get-tuple-element.321), channel_id=1, source_target_pairs={{0,1},{1,2},{2,3},{4,5},{5,6},{6,7},{8,9},{9,10},{10,11},{12,13},{... | collective-permute-start | bytes 36872 | tf_op jit(solution)/shard_map/ppermute | solution.py:17
where the time goes:
time: 166 us; the launch traced here: 165 us
  blocking collectives  121 us (73%)
  starting transfers between devices  18.7 us (11%)
  between operations  14.5 us (9%)
  local copies, waits for them, and re-layouts  9.41 us (6%)
    psum x2, blocking collectives, reverse_x(): row_total = lax.psum(pieces, 'tx')  36 us
    all_gather x2, blocking collectives, reverse_y(): strips = lax.all_gather(column_total, 'tx', axis=2, tiled=True)  27.1 us
    psum x2, blocking collectives, reverse_y(): column_total = lax.psum(pieces, 'ty')  25.1 us
    all_gather x4, blocking collectives, deliver(): gathered = lax.all_gather(strips[None], 'face', axis=0, tiled=True)  22 us
    ppermute x4, starting transfers between devices, padded(): lax.ppermute(tail, axis, [(i, (i + 1) % count) for i in range(ends)])  13.5 us
    all_gather x2, blocking collectives, reverse_x(): strips = lax.all_gather(row_total, 'ty', axis=2, tiled=True)  10.6 us
    ppermute x4, starting transfers between devices, padded(): lax.ppermute(head, axis, [((i + 1) % count, i) for i in range(ends)])  5.17 us
  transfers between devices with their start and end apart: 8, of which 0 were waited for; matrix products, arithmetic and copies ran while one was open for 3% of the time, Pallas kernels for 0%

commit v1 on v0

--- a/solution.py
+++ b/solution.py
@@ -4,6 +4,18 @@
 from jax.sharding import PartitionSpec as P
 
 STEPS = 2
+
+
+def gather_by_bits(x, axis, dim):
+    ways, here = (lax.axis_size(axis), lax.axis_index(axis))
+    grown, reach = (x, 1)
+    while reach < ways:
+        theirs = lax.ppermute(grown, axis, [(d, d ^ reach) for d in range(ways)])
+        mine_first = jnp.concatenate([grown, theirs], axis=dim)
+        theirs_first = jnp.concatenate([theirs, grown], axis=dim)
+        grown = jnp.where(here & reach == 0, mine_first, theirs_first)
+        reach = 2 * reach
+    return grown
 
 
 def padded(cells, sides, width):
@@ -86,7 +98,7 @@
     on_south = indicator(row_index == 0)
 
     def deliver(strips, parity):
-        gathered = lax.all_gather(strips[None], "face", axis=0, tiled=True)
+        gathered = gather_by_bits(strips[None], "face", 0)
         result = jnp.zeros((height_cells, width_cells, lanes_all), jnp.float32)
         for border in range(4):
             code = own_codes[border]

time: 166 us -> 160 us (0.964)
  blocking collectives: 121 us -> 100 us
  waiting for transfers between devices: 0.02 us -> 12.8 us
    all_gather x4 -> x0, blocking collectives: 22 us -> none  [deliver(): gathered = lax.all_gather(strips[None], 'face', axis=0, tiled=True)]
    ppermute x0 -> x4, waiting for transfers between devices: none -> 12.8 us  [gather_by_bits(): theirs = lax.ppermute(grown, axis, [(d, d ^ reach) for d in range(ways)])]
    ppermute x0 -> x4, starting transfers between devices: none -> 3.04 us  [gather_by_bits(): theirs = lax.ppermute(grown, axis, [(d, d ^ reach) for d in range(ways)])]
    unnamed x13 -> x16, local copies, waits for them, and re-layouts: 3.12 us -> 3.32 us
  transfers between devices with their start and end apart: 8 -> 12, of which waited for: 0 -> 3; matrix products, arithmetic and copies ran while one was open for 3% -> 1% of each run, Pallas kernels for 0% -> 0%
where the time goes in v1:
time: 160 us; the launch traced here: 159 us
  blocking collectives  100 us (62%)
  starting transfers between devices  20.1 us (13%)
  between operations  14 us (9%)
  waiting for transfers between devices  12.8 us (8%)
  local copies, waits for them, and re-layouts  10.3 us (6%)
  other arithmetic  1.87 us (1%)
    psum x2, blocking collectives, reverse_x(): row_total = lax.psum(pieces, 'tx')  35.9 us
    all_gather x2, blocking collectives, reverse_y(): strips = lax.all_gather(column_total, 'tx', axis=2, tiled=True)  26.8 us
    psum x2, blocking collectives, reverse_y(): column_total = lax.psum(pieces, 'ty')  26.6 us
    ppermute x4, waiting for transfers between devices, gather_by_bits(): theirs = lax.ppermute(grown, axis, [(d, d ^ reach) for d in range(ways)])  12.8 us
    ppermute x4, starting transfers between devices, padded(): lax.ppermute(tail, axis, [(i, (i + 1) % count) for i in range(ends)])  11.8 us
    all_gather x2, blocking collectives, reverse_x(): strips = lax.all_gather(row_total, 'ty', axis=2, tiled=True)  10.6 us
    ppermute x4, starting transfers between devices, padded(): lax.ppermute(head, axis, [((i + 1) % count, i) for i in range(ends)])  5.17 us
    unnamed x16, local copies, waits for them, and re-layouts  3.32 us
  transfers between devices with their start and end apart: 12, of which 3 were waited for; matrix products, arithmetic and copies ran while one was open for 1% of the time, Pallas kernels for 0%

profile of v1, /device:TPU:0, one launch (start us, length us, event | category | flops | bytes accessed | tf_op | source)
XLA Modules:
  0.0 159.1 jit_solution(17658043429511233421)
XLA Ops:
  0.0 0.8 copy.92
  0.8 0.8 tile.21
  1.6 0.1 tile.22
  1.7 0.6 copy-done.1
  2.5 0.7 copy-done.2
  3.2 0.1 fusion.15
  3.4 2.4 %collective-permute-start = (f32[3,8,128]{2,0,1:T(4,128)S(1)}, f32[3,8,128]{2,0,1:T(4,128)S(1)}, u32[]{:S(2)}, u32[]{:S(2)}) collective-permute-start(f32[3,8,128]{2,0,1:T(4,128)S(1)} %get-tuple-element.367), channel_id=1, source_target_pairs={{0,4},{4,8},{8,12},{1,5},{5,9},{9,13},{2,6},{6,10},{10,14},{3,7},{... | collective-permute-start | bytes 36872 | tf_op jit(solution)/shard_map/ppermute | solution.py:29
  5.8 1.3 collective-permute-start.1
  7.2 13.4 %psum.28 = f32[2,3,8,128]{3,1,2,0:T(4,128)S(1)} all-reduce(f32[2,3,8,128]{3,1,2,0:T(4,128)S(1)} %pad_maximum_fusion), channel_id=1, replica_groups=mesh['face'=2,'ty'=4,'tx'=4] {'ty'}, use_global_device_ids=true, to_apply=%region_0.1 | all-reduce | flops 6144 | bytes 49152 | tf_op jit(solution)/shard_map/psum | solution.py:172
  20.6 13.6 %all_gather.12 = f32[2,3,32,128]{3,1,2,0:T(4,128)S(1)} all-gather(f32[2,3,8,128]{3,1,2,0:T(4,128)S(1)} %psum.28), channel_id=1, replica_groups=mesh['face'=2,'ty'=4,'tx'=4] {'tx'}, dimensions={2}, use_global_device_ids=true | all-gather | bytes 122880 | tf_op jit(solution)/shard_map/all_gather | solution.py:173
  34.2 1.5 collective-permute-start.2
  35.7 0.7 copy-done.5
  36.4 0.6 fusion.67
  38.3 0.7 fusion.66
  48.0 0.7 copy-done.3
  51.6 0.1 scatter-add.80
  51.8 0.1 scatter-add.81
  52.3 0.1 scatter-add.85
  52.5 0.1 scatter-add.89
  52.9 3.5 %collective-permute-start.3 = (f32[8,3,128]{2,0,1:T(8,128)S(1)}, f32[8,3,128]{2,0,1:T(8,128)S(1)}, u32[]{:S(2)}, u32[]{:S(2)}) collective-permute-start(f32[8,3,128]{2,0,1:T(8,128)S(1)} %get-tuple-element.339), channel_id=1, source_target_pairs={{0,1},{1,2},{2,3},{4,5},{5,6},{6,7},{8,9},{9,10},{10,11},{12,13},{... | collective-permute-start | bytes 36872 | tf_op jit(solution)/shard_map/ppermute | solution.py:29
  56.5 1.3 collective-permute-start.4
  57.8 20.2 %psum.29 = f32[2,3,8,128]{3,2,1,0:T(8,128)S(1)} all-reduce(f32[2,3,8,128]{3,2,1,0:T(8,128)S(1)} %pad_maximum_fusion.1), channel_id=1, replica_groups=mesh['face'=2,'ty'=4,'tx'=4] {'tx'}, use_global_device_ids=true, to_apply=%region_1.2 | all-reduce | flops 6144 | bytes 49152 | tf_op jit(solution)/shard_map/psum | solution.py:151
  78.0 5.3 %all_gather.13 = f32[2,3,32,128]{3,2,1,0:T(8,128)S(1)} all-gather(f32[2,3,8,128]{3,2,1,0:T(8,128)S(1)} %psum.29), channel_id=1, replica_groups=mesh['face'=2,'ty'=4,'tx'=4] {'ty'}, dimensions={2}, use_global_device_ids=true | all-gather | bytes 122880 | tf_op jit(solution)/shard_map/all_gather | solution.py:152
  83.3 0.5 collective-permute-start.5
  83.8 4.5 %collective-permute-done.5 = f32[1,2,3,32,128]{4,3,2,1,0:T(8,128)S(1)} collective-permute-done((f32[1,2,3,32,128]{4,3,2,1,0:T(8,128)S(1)}, f32[1,2,3,32,128]{4,3,2,1,0:T(8,128)S(1)}, u32[]{:S(2)}, u32[]{:S(2)}) %collective-permute-start.5) | collective-permute-done | bytes 98336 | tf_op jit(solution)/shard_map/ppermute | solution.py:13
  88.7 0.1 scatter-add.95
  88.8 0.1 scatter-add.99
  89.6 0.6 copy-done
  90.2 0.7 slice-done
  91.0 1.4 collective-permute-start.6
  92.4 1.3 collective-permute-start.7
  93.7 13.2 %psum.30 = f32[2,3,8,128]{3,2,1,0:T(8,128)S(1)} all-reduce(f32[2,3,8,128]{3,2,1,0:T(8,128)S(1)} %pad_maximum_fusion.2), channel_id=1, replica_groups=mesh['face'=2,'ty'=4,'tx'=4] {'ty'}, use_global_device_ids=true, to_apply=%region_2.3 | all-reduce | flops 6144 | bytes 49152 | tf_op jit(solution)/shard_map/psum | solution.py:172
  106.9 13.2 %all_gather.14 = f32[2,3,32,128]{3,2,1,0:T(8,128)S(1)} all-gather(f32[2,3,8,128]{3,2,1,0:T(8,128)S(1)} %psum.30), channel_id=1, replica_groups=mesh['face'=2,'ty'=4,'tx'=4] {'tx'}, dimensions={2}, use_global_device_ids=true | all-gather | bytes 122880 | tf_op jit(solution)/shard_map/all_gather | solution.py:173
  120.2 0.5 collective-permute-start.8
  120.7 0.1 scatter-add.100
  120.9 0.1 scatter-add.101
  121.0 3.8 %collective-permute-done.8 = f32[1,2,3,32,128]{4,3,2,1,0:T(8,128)S(1)} collective-permute-done((f32[1,2,3,32,128]{4,3,2,1,0:T(8,128)S(1)}, f32[1,2,3,32,128]{4,3,2,1,0:T(8,128)S(1)}, u32[]{:S(2)}, u32[]{:S(2)}) %collective-permute-start.8) | collective-permute-done | bytes 98336 | tf_op jit(solution)/shard_map/ppermute | solution.py:13
  125.1 0.1 scatter-add.105
  125.3 0.1 scatter-add.109
  125.7 1.3 collective-permute-start.10
  127.1 4.5 %collective-permute-start.9 = (f32[8,3,128]{2,0,1:T(8,128)S(1)}, f32[8,3,128]{2,0,1:T(8,128)S(1)}, u32[]{:S(2)}, u32[]{:S(2)}) collective-permute-start(f32[8,3,128]{2,0,1:T(8,128)S(1)} %get-tuple-element.329), channel_id=1, source_target_pairs={{0,1},{1,2},{2,3},{4,5},{5,6},{6,7},{8,9},{9,10},{10,11},{12,13},{... | collective-permute-start | bytes 36872 | tf_op jit(solution)/shard_map/ppermute | solution.py:29
  131.6 15.8 %psum.31 = f32[2,3,8,128]{3,2,1,0:T(8,128)S(1)} all-reduce(f32[2,3,8,128]{3,2,1,0:T(8,128)S(1)} %pad_maximum_fusion.3), channel_id=1, replica_groups=mesh['face'=2,'ty'=4,'tx'=4] {'tx'}, use_global_device_ids=true, to_apply=%region_3.4 | all-reduce | flops 6144 | bytes 49152 | tf_op jit(solution)/shard_map/psum | solution.py:151
  147.4 5.3 %all_gather.15 = f32[2,3,32,128]{3,2,1,0:T(8,128)S(1)} all-gather(f32[2,3,8,128]{3,2,1,0:T(8,128)S(1)} %psum.31), channel_id=1, replica_groups=mesh['face'=2,'ty'=4,'tx'=4] {'ty'}, dimensions={2}, use_global_device_ids=true | all-gather | bytes 122880 | tf_op jit(solution)/shard_map/all_gather | solution.py:152
  152.7 0.5 collective-permute-start.11
  153.3 4.5 %collective-permute-done.11 = f32[1,2,3,32,128]{4,3,2,1,0:T(8,128)S(1)} collective-permute-done((f32[1,2,3,32,128]{4,3,2,1,0:T(8,128)S(1)}, f32[1,2,3,32,128]{4,3,2,1,0:T(8,128)S(1)}, u32[]{:S(2)}, u32[]{:S(2)}) %collective-permute-start.11) | collective-permute-done | bytes 98336 | tf_op jit(solution)/shard_map/ppermute | solution.py:13
  158.1 0.1 scatter-add.115
  158.3 0.1 scatter-add.119
  158.4 0.6 copy.129
  (144 shorter events, 2.9 us)
Async XLA Ops:
  1.6 0.8 copy-start.1
  2.5 0.7 copy-start.2
  3.4 48.2 %collective-permute-start = (f32[3,8,128]{2,0,1:T(4,128)S(1)}, f32[3,8,128]{2,0,1:T(4,128)S(1)}, u32[]{:S(2)}, u32[]{:S(2)}) collective-permute-start(f32[3,8,128]{2,0,1:T(4,128)S(1)} %get-tuple-element.367), channel_id=1, source_target_pairs={{0,4},{4,8},{8,12},{1,5},{5,9},{9,13},{2,6},{6,10},{10,14},{3,7},{... | collective-permute-start | bytes 36872 | tf_op jit(solution)/shard_map/ppermute | solution.py:29
  5.8 46.0 %collective-permute-start.1 = (f32[3,8,128]{2,0,1:T(4,128)S(1)}, f32[3,8,128]{2,0,1:T(4,128)S(1)}, u32[]{:S(2)}, u32[]{:S(2)}) collective-permute-start(f32[3,8,128]{2,0,1:T(4,128)S(1)} %get-tuple-element.366), channel_id=1, source_target_pairs={{4,0},{8,4},{12,8},{5,1},{9,5},{13,9},{6,2},{10,6},{14,10},{7,3},{... | collective-permute-start | bytes 36872 | tf_op jit(solution)/shard_map/ppermute | solution.py:31
  34.2 17.8 %collective-permute-start.2 = (f32[1,2,3,32,128]{4,2,3,1,0:T(4,128)S(1)}, f32[1,2,3,32,128]{4,2,3,1,0:T(4,128)S(1)}, u32[]{:S(2)}, u32[]{:S(2)}) collective-permute-start(f32[1,2,3,32,128]{4,2,3,1,0:T(4,128)S(1)} %bitcast.117), channel_id=1, source_target_pairs={{0,16},{16,0},{1,17},{17,1},{2,18},{18,2},{3,19},{19,3},{4,20},{20... | collective-permute-start | bytes 294920 | tf_op jit(solution)/shard_map/ppermute | solution.py:13
  35.7 0.7 copy-start.5
  35.7 0.7 copy-start.6
  48.0 0.8 copy-start.3
  50.8 0.7 copy-start.4
  52.9 30.8 %collective-permute-start.3 = (f32[8,3,128]{2,0,1:T(8,128)S(1)}, f32[8,3,128]{2,0,1:T(8,128)S(1)}, u32[]{:S(2)}, u32[]{:S(2)}) collective-permute-start(f32[8,3,128]{2,0,1:T(8,128)S(1)} %get-tuple-element.339), channel_id=1, source_target_pairs={{0,1},{1,2},{2,3},{4,5},{5,6},{6,7},{8,9},{9,10},{10,11},{12,13},{... | collective-permute-start | bytes 36872 | tf_op jit(solution)/shard_map/ppermute | solution.py:29
  56.5 27.3 %collective-permute-start.4 = (f32[8,3,128]{2,0,1:T(8,128)S(1)}, f32[8,3,128]{2,0,1:T(8,128)S(1)}, u32[]{:S(2)}, u32[]{:S(2)}) collective-permute-start(f32[8,3,128]{2,0,1:T(8,128)S(1)} %get-tuple-element.311), channel_id=1, source_target_pairs={{1,0},{2,1},{3,2},{5,4},{6,5},{7,6},{9,8},{10,9},{11,10},{13,12},{... | collective-permute-start | bytes 36872 | tf_op jit(solution)/shard_map/ppermute | solution.py:31
  83.3 5.0 %collective-permute-start.5 = (f32[1,2,3,32,128]{4,3,2,1,0:T(8,128)S(1)}, f32[1,2,3,32,128]{4,3,2,1,0:T(8,128)S(1)}, u32[]{:S(2)}, u32[]{:S(2)}) collective-permute-start(f32[1,2,3,32,128]{4,3,2,1,0:T(8,128)S(1)} %bitcast.121), channel_id=1, source_target_pairs={{0,16},{16,0},{1,17},{17,1},{2,18},{18,2},{3,19},{19,3},{4,20},{20... | collective-permute-start | bytes 294920 | tf_op jit(solution)/shard_map/ppermute | solution.py:13
  89.6 0.6 copy-start
  90.2 0.8 slice-start
  91.0 29.7 %collective-permute-start.6 = (f32[3,8,128]{2,0,1:T(4,128)S(1)}, f32[3,8,128]{2,0,1:T(4,128)S(1)}, u32[]{:S(2)}, u32[]{:S(2)}) collective-permute-start(f32[3,8,128]{2,0,1:T(4,128)S(1)} %get-tuple-element.372), channel_id=1, source_target_pairs={{0,4},{4,8},{8,12},{1,5},{5,9},{9,13},{2,6},{6,10},{10,14},{3,7},{... | collective-permute-start | bytes 36872 | tf_op jit(solution)/shard_map/ppermute | solution.py:29
  92.4 28.5 %collective-permute-start.7 = (f32[3,8,128]{2,0,1:T(4,128)S(1)}, f32[3,8,128]{2,0,1:T(4,128)S(1)}, u32[]{:S(2)}, u32[]{:S(2)}) collective-permute-start(f32[3,8,128]{2,0,1:T(4,128)S(1)} %copy.118), channel_id=1, source_target_pairs={{4,0},{8,4},{12,8},{5,1},{9,5},{13,9},{6,2},{10,6},{14,10},{7,3},{... | collective-permute-start | bytes 36872 | tf_op jit(solution)/shard_map/ppermute | solution.py:31
  120.2 4.6 %collective-permute-start.8 = (f32[1,2,3,32,128]{4,3,2,1,0:T(8,128)S(1)}, f32[1,2,3,32,128]{4,3,2,1,0:T(8,128)S(1)}, u32[]{:S(2)}, u32[]{:S(2)}) collective-permute-start(f32[1,2,3,32,128]{4,3,2,1,0:T(8,128)S(1)} %bitcast.123), channel_id=1, source_target_pairs={{0,16},{16,0},{1,17},{17,1},{2,18},{18,2},{3,19},{19,3},{4,20},{20... | collective-permute-start | bytes 294920 | tf_op jit(solution)/shard_map/ppermute | solution.py:13
  125.7 27.5 %collective-permute-start.10 = (f32[8,3,128]{2,0,1:T(8,128)S(1)}, f32[8,3,128]{2,0,1:T(8,128)S(1)}, u32[]{:S(2)}, u32[]{:S(2)}) collective-permute-start(f32[8,3,128]{2,0,1:T(8,128)S(1)} %get-tuple-element.295), channel_id=1, source_target_pairs={{1,0},{2,1},{3,2},{5,4},{6,5},{7,6},{9,8},{10,9},{11,10},{13,12},{... | collective-permute-start | bytes 36872 | tf_op jit(solution)/shard_map/ppermute | solution.py:31
  127.1 26.2 %collective-permute-start.9 = (f32[8,3,128]{2,0,1:T(8,128)S(1)}, f32[8,3,128]{2,0,1:T(8,128)S(1)}, u32[]{:S(2)}, u32[]{:S(2)}) collective-permute-start(f32[8,3,128]{2,0,1:T(8,128)S(1)} %get-tuple-element.329), channel_id=1, source_target_pairs={{0,1},{1,2},{2,3},{4,5},{5,6},{6,7},{8,9},{9,10},{10,11},{12,13},{... | collective-permute-start | bytes 36872 | tf_op jit(solution)/shard_map/ppermute | solution.py:29
  152.7 5.0 %collective-permute-start.11 = (f32[1,2,3,32,128]{4,3,2,1,0:T(8,128)S(1)}, f32[1,2,3,32,128]{4,3,2,1,0:T(8,128)S(1)}, u32[]{:S(2)}, u32[]{:S(2)}) collective-permute-start(f32[1,2,3,32,128]{4,3,2,1,0:T(8,128)S(1)} %bitcast.119), channel_id=1, source_target_pairs={{0,16},{16,0},{1,17},{17,1},{2,18},{18,2},{3,19},{19,3},{4,20},{20... | collective-permute-start | bytes 294920 | tf_op jit(solution)/shard_map/ppermute | solution.py:13
